TPU v7x, 32 devices: a whole 2x2x4 slice. The times are simulated.
32 devices in a mesh: view: 4 (over x, core), bx: 4 (over z), by: 2 (over y).
Axes of the slice: x: 2, y: 2, z: 4, core: 2. Of those that a mesh axis runs over, the one named last changes fastest.
Arguments:
- estimate: float32 [256, 32, 128], P('bx', 'by'), may hold values from 0.5 to 2
- observed: float32 [4, 2048, 512], P('view', ('bx', 'by')), may hold values from 0.25 to 4
- destination: int32 [4, 2048, 1], P('view', ('bx', 'by')), may hold values from 0 to 7; in each aligned block of 256 rows (0 to 255, 256 to 511, ..., all dimensions but the last counted through in order) at most 64 rows name the same one
- slot_index: int32 [4, 2048], P('view', ('bx', 'by')), may hold values from 0 to 255
- valid_count: int32 [4, 2048], P('view', ('bx', 'by')), may hold values from 32 to 128
- blend_weight: float32 [4, 2048], P('view', ('bx', 'by')), may hold values from 0.2 to 1
- kernel_x: float32 [4, 17], P('view'), may hold values from 0.1 to 1
- kernel_y: float32 [4, 17], P('view'), may hold values from 0.1 to 1
- kernel_z: float32 [4, 33], P('view'), may hold values from 0.1 to 1
Outputs:
- updated: float32 [256, 32, 128], P('bx', 'by')
Inputs may be any that keep to these rules, and one draw needn't show every extreme that they name: `destination`: in each view, the 256 rows of one device name no brick more than 64 times, a bound that some block reaches.
All inputs are finite; a program needn't handle non-finite values.
Results may differ from a plain program's by a relative error of at most 0.0001.
Values sent between devices are 32-bit elements; how exact they have to be, the bound alone decides.
No kernel may reach another device: no remote copies, remote signals or barrier semaphores. Data moves between devices by JAX's collectives and lax.ppermute only.
A program may use at most 64 MiB of HBM per device.

v0:
```python
import jax
import jax.numpy as jnp
from jax import lax
from jax.sharding import PartitionSpec as P

R = 8
RZ = 16
YP = 4
PV = 512
SLOTS = 256
PIECES = 256
PRIOR_WEIGHT = 0.5


def with_halo(block, sides, width):
    for axis, dim in sides:
        count = lax.axis_size(axis)
        forward = [(i, i + 1) for i in range(count - 1)]
        backward = [(target, source) for source, target in forward]
        low = lax.ppermute(
            lax.slice_in_dim(block, block.shape[dim] - width, None, axis=dim), axis, forward
        )
        high = lax.ppermute(lax.slice_in_dim(block, 0, width, axis=dim), axis, backward)
        block = jnp.concatenate([low, block, high], axis=dim)
    return block


def band_matrix(kernel, extent, radius):
    spread = jnp.arange(extent + 2 * radius)[None, :] - jnp.arange(extent)[:, None]
    offsets = jnp.arange(2 * radius + 1)
    hits = (spread[:, :, None] == offsets[None, None, :]).astype(jnp.float32)
    return jnp.sum(kernel[None, None, :] * hits, axis=2)


def separable(padded, kernel_a, kernel_b, kernel_c):
    rows_x = padded.shape[0] - 2 * R
    rows_y = padded.shape[1] - 2 * R
    depth_cells = padded.shape[2]
    along_first = jnp.einsum(
        "xe,eyz->xyz", band_matrix(kernel_a, rows_x, R), padded, precision=lax.Precision.HIGHEST
    )
    second = jnp.einsum(
        "ye,xez->xyz",
        band_matrix(kernel_b, rows_y, R),
        along_first,
        precision=lax.Precision.HIGHEST,
    )
    depth_band = band_matrix(kernel_c, depth_cells, RZ)[:, RZ : RZ + depth_cells]
    return jnp.einsum("zw,xyw->xyz", depth_band, second, precision=lax.Precision.HIGHEST)


def local(
    estimate,
    observed,
    destination,
    slot_index,
    valid_count,
    blend_weight,
    kernel_x,
    kernel_y,
    kernel_z,
):
    rows_x, rows_y, depth_cells = estimate.shape
    norm_x = kernel_x[0] / jnp.sum(kernel_x[0])
    norm_y = kernel_y[0] / jnp.sum(kernel_y[0])
    norm_z = kernel_z[0] / jnp.sum(kernel_z[0])
    padded = with_halo(estimate, (("bx", 0), ("by", 1)), R)
    blurred = separable(padded, norm_x, norm_y, norm_z)
    count_bx = lax.axis_size("bx")
    count_by = lax.axis_size("by")
    bricks = count_bx * count_by
    capacity = max(4, 2 * PIECES // bricks)
    target = destination[0, :, 0]
    member = (target[:, None] == jnp.arange(bricks)[None, :]).astype(jnp.int32)
    slot_rank = jnp.sum((jnp.cumsum(member, axis=0) - 1) * member, axis=1)
    send_place = target * capacity + slot_rank
    send_rows = jnp.zeros((bricks * capacity, PV), jnp.float32).at[send_place].set(observed[0])
    send_meta = (
        jnp.zeros((bricks * capacity, 2), jnp.int32)
        .at[send_place]
        .set(jnp.stack([slot_index[0], valid_count[0]], axis=1))
    )
    send_weight = jnp.zeros((bricks * capacity,), jnp.float32).at[send_place].set(blend_weight[0])
    recv_rows, recv_meta, recv_weight = (
        lax.all_to_all(
            send_rows.reshape(bricks, capacity, PV),
            ("bx", "by"),
            split_axis=0,
            concat_axis=0,
            tiled=True,
        ),
        lax.all_to_all(
            send_meta.reshape(bricks, capacity, 2),
            ("bx", "by"),
            split_axis=0,
            concat_axis=0,
            tiled=True,
        ),
        lax.all_to_all(
            send_weight.reshape(bricks, capacity),
            ("bx", "by"),
            split_axis=0,
            concat_axis=0,
            tiled=True,
        ),
    )
    recv_rows = recv_rows.reshape(bricks * capacity, PV)
    recv_meta = recv_meta.reshape(bricks * capacity, 2)
    recv_weight = recv_weight.reshape(bricks * capacity)
    depth_index = jnp.arange(depth_cells, dtype=jnp.int32)
    keep_mask = (depth_index[None, :] < recv_meta[:, 1:2]).astype(jnp.float32) * recv_weight[
        :, None
    ]
    weighted = (recv_rows.reshape(-1, YP, depth_cells) * keep_mask[:, None, :]).reshape(-1, PV)
    chooser = (jnp.arange(SLOTS)[:, None] == recv_meta[:, 0][None, :]).astype(jnp.float32)
    data_slots = jnp.dot(chooser, weighted, precision=lax.Precision.HIGHEST)
    cover_slots = jnp.dot(chooser, keep_mask, precision=lax.Precision.HIGHEST)
    data_volume = data_slots.reshape(rows_x, rows_y, depth_cells)
    cover_wide = jnp.broadcast_to(
        cover_slots.reshape(rows_x, rows_y // YP, 1, depth_cells),
        (rows_x, rows_y // YP, YP, depth_cells),
    )
    cover_volume = cover_wide.reshape(rows_x, rows_y, depth_cells)
    ratio_field = (data_volume + PRIOR_WEIGHT * blurred) / ((cover_volume + PRIOR_WEIGHT) * blurred)
    padded_ratio = with_halo(ratio_field, (("bx", 0), ("by", 1)), R)
    correction = separable(padded_ratio, norm_x[::-1], norm_y[::-1], norm_z[::-1])
    log_term = jnp.log(correction)
    logsum = lax.psum(log_term, "view")
    return estimate * jnp.exp(logsum)


def solution(mesh):
    placed = (
        P("bx", "by", None),
        P("view", ("bx", "by"), None),
        P("view", ("bx", "by"), None),
        P("view", ("bx", "by")),
        P("view", ("bx", "by")),
        P("view", ("bx", "by")),
        P("view", None),
        P("view", None),
        P("view", None),
    )
    return jax.shard_map(
        local, mesh=mesh, in_specs=placed, out_specs=P("bx", "by", None), check_vma=False
    )
```

profile of v0, /device:TPU:0, one launch (start us, length us, event | category | flops | bytes accessed | tf_op | source)
XLA Modules:
  0.0 148.1 jit_solution(831064255658808431)
XLA Ops:
  6.5 0.7 fusion.26
  8.1 0.8 fusion.23
  8.9 0.7 compare_select_fusion
  9.6 1.6 %scatter_custom_fusion.2 = f32[512]{0:T(512)S(1)} fusion(s32[256]{0:T(256)S(1)} %bitcast.81, f32[256]{0:T(256)} %bitcast.89, f32[]{:T(128)} %constant.22.clone.1), kind=kCustom, calls=%fused_computation.64 | custom fusion | bytes 2560 | tf_op jit(solution)/shard_map/scatter | solution.py:83
  11.1 0.7 all_to_all.14
  11.8 7.3 %all-to-all-start.2 = ((f32[8,1,64]{2,1,0:T(1,128)}), f32[8,1,64]{2,1,0:T(1,128)S(1)}, u32[]{:S(2)}, u32[]{:S(2)}) async-start(f32[8,1,64]{2,1,0:T(1,128)} %all_to_all.14), calls=%async_computation.2 | async-start | bytes 8192 | tf_op jit(solution)/shard_map/all_to_all | solution.py:99
  19.1 0.9 fusion.34
  20.0 3.9 %collective-permute-start = (f32[8,16,128]{2,0,1:T(8,128)S(1)}, f32[8,16,128]{2,0,1:T(8,128)S(1)}, u32[]{:S(2)}, u32[]{:S(2)}) collective-permute-start(f32[8,16,128]{2,0,1:T(8,128)S(1)} %copy.60), channel_id=1, source_target_pairs={{0,2},{2,4},{4,6},{1,3},{3,5},{5,7},{8,10},{10,12},{12,14},{9,11},... | collective-permute-start | bytes 196616 | tf_op jit(solution)/shard_map/ppermute | solution.py:20
  24.0 1.3 collective-permute-start.1
  25.3 1.3 reduce_sum.92
  26.6 0.7 reverse.9
  27.3 1.3 reduce_sum.97
  28.6 0.7 reverse.10
  29.3 1.3 reduce_sum.99
  30.6 0.7 reverse.11
  31.4 1.3 broadcast_divide_fusion.4
  32.7 1.2 broadcast_divide_fusion.2
  33.9 1.3 broadcast_divide_fusion
  36.0 0.7 pad_add_fusion
  36.8 1.2 scatter_custom_fusion
  38.2 0.7 reshape.213
  38.9 6.6 %all-to-all-start = ((s32[8,1,128]{2,1,0:T(1,128)}), s32[8,1,128]{2,1,0:T(1,128)S(1)}, u32[]{:S(2)}, u32[]{:S(2)}) async-start(s32[8,1,128]{2,1,0:T(1,128)} %reshape.213), calls=%async_computation | async-start | bytes 8192 | tf_op jit(solution)/shard_map/all_to_all | solution.py:92
  45.6 2.5 %scatter_custom_fusion.1 = f32[512,512]{1,0:T(8,128)} fusion(s32[256]{0:T(256)S(1)} %bitcast.83, f32[1,256,512]{2,1,0:T(8,128)S(1)} %copy-done, f32[]{:T(128)} %constant.22.clone.1), kind=kCustom, calls=%fused_computation.28 | custom fusion | bytes 1572868 | tf_op jit(solution)/shard_map/scatter | solution.py:77
  48.7 0.7 reduce.8
  49.5 2.5 %all-to-all-done = s32[8,1,128]{2,1,0:T(1,128)S(1)} async-done(((s32[8,1,128]{2,1,0:T(1,128)}), s32[8,1,128]{2,1,0:T(1,128)S(1)}, u32[]{:S(2)}, u32[]{:S(2)}) %all-to-all-start) | async-done | bytes 4128 | tf_op jit(solution)/shard_map/all_to_all | solution.py:92
  51.9 3.6 %all-to-all-start.1 = ((f32[8,64,512]{2,1,0:T(8,128)}), f32[8,64,512]{2,1,0:T(8,128)S(1)}, u32[]{:S(2)}, u32[]{:S(2)}) async-start(f32[8,64,512]{2,1,0:T(8,128)} %bitcast.14), calls=%async_computation.1 | async-start | bytes 2097152 | tf_op jit(solution)/shard_map/all_to_all | solution.py:85
  56.0 0.7 reduce.9
  57.1 3.9 %collective-permute-start.2 = (f32[80,8,128]{2,0,1:T(8,128)S(1)}, f32[80,8,128]{2,0,1:T(8,128)S(1)}, u32[]{:S(2)}, u32[]{:S(2)}) collective-permute-start(f32[80,8,128]{2,0,1:T(8,128)S(1)} %get-tuple-element.13), channel_id=1, source_target_pairs={{0,1},{2,3},{4,5},{6,7},{8,9},{10,11},{12,13},{14,15},{16,17},{18,... | collective-permute-start | bytes 983048 | tf_op jit(solution)/shard_map/ppermute | solution.py:20
  61.0 1.3 collective-permute-start.3
  63.1 7.8 %collective-permute-done.2 = f32[80,8,128]{2,0,1:T(8,128)S(1)} collective-permute-done((f32[80,8,128]{2,0,1:T(8,128)S(1)}, f32[80,8,128]{2,0,1:T(8,128)S(1)}, u32[]{:S(2)}, u32[]{:S(2)}) %collective-permute-start.2) | collective-permute-done | bytes 327712 | tf_op jit(solution)/shard_map/ppermute | solution.py:20
  70.8 4.3 %collective-permute-done.3 = f32[80,8,128]{2,0,1:T(8,128)S(1)} collective-permute-done((f32[80,8,128]{2,0,1:T(8,128)S(1)}, f32[80,8,128]{2,0,1:T(8,128)S(1)}, u32[]{:S(2)}, u32[]{:S(2)}) %collective-permute-start.3) | collective-permute-done | bytes 327712 | tf_op jit(solution)/shard_map/ppermute | solution.py:23
  75.2 1.0 fusion
  76.2 1.3 convolution_bitcast_fusion.1
  77.5 2.3 %all-to-all-done.1 = f32[8,64,512]{2,1,0:T(8,128)S(1)} async-done(((f32[8,64,512]{2,1,0:T(8,128)}), f32[8,64,512]{2,1,0:T(8,128)S(1)}, u32[]{:S(2)}, u32[]{:S(2)}) %all-to-all-start.1) | async-done | bytes 1048608 | tf_op jit(solution)/shard_map/all_to_all | solution.py:85
  79.9 0.7 fusion.8
  80.8 0.6 multiply_divide_fusion
  81.5 1.7 %collective-permute-start.4 = (f32[8,16,128]{2,1,0:T(8,128)S(1)}, f32[8,16,128]{2,1,0:T(8,128)S(1)}, u32[]{:S(2)}, u32[]{:S(2)}) collective-permute-start(f32[8,16,128]{2,1,0:T(8,128)S(1)} %get-tuple-element.15), channel_id=1, source_target_pairs={{0,2},{2,4},{4,6},{1,3},{3,5},{5,7},{8,10},{10,12},{12,14},{9,11},... | collective-permute-start | bytes 196616 | tf_op jit(solution)/shard_map/ppermute | solution.py:20
  83.2 1.3 collective-permute-start.5
  85.1 4.3 %collective-permute-done.5 = f32[8,16,128]{2,1,0:T(8,128)S(1)} collective-permute-done((f32[8,16,128]{2,1,0:T(8,128)S(1)}, f32[8,16,128]{2,1,0:T(8,128)S(1)}, u32[]{:S(2)}, u32[]{:S(2)}) %collective-permute-start.5) | collective-permute-done | bytes 65568 | tf_op jit(solution)/shard_map/ppermute | solution.py:23
  89.4 2.7 %collective-permute-start.6 = (f32[80,8,128]{2,1,0:T(8,128)S(1)}, f32[80,8,128]{2,1,0:T(8,128)S(1)}, u32[]{:S(2)}, u32[]{:S(2)}) collective-permute-start(f32[80,8,128]{2,1,0:T(8,128)S(1)} %get-tuple-element.11), channel_id=1, source_target_pairs={{0,1},{2,3},{4,5},{6,7},{8,9},{10,11},{12,13},{14,15},{16,17},{18,... | collective-permute-start | bytes 983048 | tf_op jit(solution)/shard_map/ppermute | solution.py:20
  92.2 1.5 collective-permute-start.7
  93.6 3.5 %collective-permute-done.6 = f32[80,8,128]{2,1,0:T(8,128)S(1)} collective-permute-done((f32[80,8,128]{2,1,0:T(8,128)S(1)}, f32[80,8,128]{2,1,0:T(8,128)S(1)}, u32[]{:S(2)}, u32[]{:S(2)}) %collective-permute-start.6) | collective-permute-done | bytes 327712 | tf_op jit(solution)/shard_map/ppermute | solution.py:20
  97.1 4.1 %collective-permute-done.7 = f32[80,8,128]{2,1,0:T(8,128)S(1)} collective-permute-done((f32[80,8,128]{2,1,0:T(8,128)S(1)}, f32[80,8,128]{2,1,0:T(8,128)S(1)}, u32[]{:S(2)}, u32[]{:S(2)}) %collective-permute-start.7) | collective-permute-done | bytes 327712 | tf_op jit(solution)/shard_map/ppermute | solution.py:23
  101.4 1.8 %fusion.6 = f32[64,32,128]{2,0,1:T(8,128)S(1)} fusion(f32[80,32,128]{2,1,0:T(8,128)S(1)} %pad_maximum_fusion, f32[64,80]{1,0:T(8,128)S(1)} %get-tuple-element.7), kind=kOutput, calls=%fused_computation.13 | convolution fusion | flops 251658240 | bytes 2379776 | tf_op jit(solution)/shard_map/xe,eyz->xyz/dot_general | solution.py:39
  103.1 1.3 convolution_bitcast_fusion
  104.4 1.4 convolution_log_fusion
  105.8 33.5 %all-reduce.2.cloned.1.call-done = f32[64,16,128]{2,1,0:T(8,128)} async-done(((f32[64,16,128]{2,1,0:T(8,128)}), f32[64,16,128]{2,1,0:T(8,128)}) %all-reduce.2.cloned.1.call-update) | async-done | bytes 524304 | tf_op jit(solution)/shard_map/psum | solution.py:128
  139.3 1.9 %exponential_multiply_fusion = f32[64,16,128]{2,1,0:T(8,128)} fusion(f32[64,16,128]{2,1,0:T(8,128)S(1)} %copy-done.1, f32[64,16,128]{2,1,0:T(8,128)} %all-reduce.2.cloned.1.call-done), kind=kLoop, calls=%fused_computation.30 | loop fusion | flops 131072 | bytes 1572864 | tf_op jit(solution)/shard_map/mul | solution.py:129
  (44 shorter events, 5.5 us)
Async XLA Ops:
  6.5 39.1 %copy-start = (f32[1,256,512]{2,1,0:T(8,128)S(1)}, f32[1,256,512]{2,1,0:T(8,128)}, u32[]{:S(2)}) copy-start(f32[1,256,512]{2,1,0:T(8,128)} %param.10) | copy-start | bytes 1572868
  11.8 27.1 %all-to-all-start.2 = ((f32[8,1,64]{2,1,0:T(1,128)}), f32[8,1,64]{2,1,0:T(1,128)S(1)}, u32[]{:S(2)}, u32[]{:S(2)}) async-start(f32[8,1,64]{2,1,0:T(1,128)} %all_to_all.14), calls=%async_computation.2 | async-start | bytes 8192 | tf_op jit(solution)/shard_map/all_to_all | solution.py:99
  20.0 36.9 %collective-permute-start = (f32[8,16,128]{2,0,1:T(8,128)S(1)}, f32[8,16,128]{2,0,1:T(8,128)S(1)}, u32[]{:S(2)}, u32[]{:S(2)}) collective-permute-start(f32[8,16,128]{2,0,1:T(8,128)S(1)} %copy.60), channel_id=1, source_target_pairs={{0,2},{2,4},{4,6},{1,3},{3,5},{5,7},{8,10},{10,12},{12,14},{9,11},... | collective-permute-start | bytes 196616 | tf_op jit(solution)/shard_map/ppermute | solution.py:20
  24.0 33.1 %collective-permute-start.1 = (f32[8,16,128]{2,0,1:T(8,128)S(1)}, f32[8,16,128]{2,0,1:T(8,128)S(1)}, u32[]{:S(2)}, u32[]{:S(2)}) collective-permute-start(f32[8,16,128]{2,0,1:T(8,128)S(1)} %copy.61), channel_id=1, source_target_pairs={{2,0},{4,2},{6,4},{3,1},{5,3},{7,5},{10,8},{12,10},{14,12},{11,9},... | collective-permute-start | bytes 196616 | tf_op jit(solution)/shard_map/ppermute | solution.py:23
  38.9 13.0 %all-to-all-start = ((s32[8,1,128]{2,1,0:T(1,128)}), s32[8,1,128]{2,1,0:T(1,128)S(1)}, u32[]{:S(2)}, u32[]{:S(2)}) async-start(s32[8,1,128]{2,1,0:T(1,128)} %reshape.213), calls=%async_computation | async-start | bytes 8192 | tf_op jit(solution)/shard_map/all_to_all | solution.py:92
  48.1 8.8 %copy-start.1 = (f32[64,16,128]{2,1,0:T(8,128)S(1)}, f32[64,16,128]{2,1,0:T(8,128)}, u32[]{:S(2)}) copy-start(f32[64,16,128]{2,1,0:T(8,128)} %param.9) | copy-start | bytes 1572868
  51.9 27.9 %all-to-all-start.1 = ((f32[8,64,512]{2,1,0:T(8,128)}), f32[8,64,512]{2,1,0:T(8,128)S(1)}, u32[]{:S(2)}, u32[]{:S(2)}) async-start(f32[8,64,512]{2,1,0:T(8,128)} %bitcast.14), calls=%async_computation.1 | async-start | bytes 2097152 | tf_op jit(solution)/shard_map/all_to_all | solution.py:85
  55.5 83.9 %all-reduce.2.cloned.1.call-start = ((), (), s32[]{:S(2)}) async-start(), calls=%async_computation.3 | async-start | bytes 1048576 | tf_op jit(solution)/shard_map/psum | solution.py:128
  57.1 13.7 %collective-permute-start.2 = (f32[80,8,128]{2,0,1:T(8,128)S(1)}, f32[80,8,128]{2,0,1:T(8,128)S(1)}, u32[]{:S(2)}, u32[]{:S(2)}) collective-permute-start(f32[80,8,128]{2,0,1:T(8,128)S(1)} %get-tuple-element.13), channel_id=1, source_target_pairs={{0,1},{2,3},{4,5},{6,7},{8,9},{10,11},{12,13},{14,15},{16,17},{18,... | collective-permute-start | bytes 983048 | tf_op jit(solution)/shard_map/ppermute | solution.py:20
  61.0 14.1 %collective-permute-start.3 = (f32[80,8,128]{2,0,1:T(8,128)S(1)}, f32[80,8,128]{2,0,1:T(8,128)S(1)}, u32[]{:S(2)}, u32[]{:S(2)}) collective-permute-start(f32[80,8,128]{2,0,1:T(8,128)S(1)} %get-tuple-element.14), channel_id=1, source_target_pairs={{1,0},{3,2},{5,4},{7,6},{9,8},{11,10},{13,12},{15,14},{17,16},{19,... | collective-permute-start | bytes 983048 | tf_op jit(solution)/shard_map/ppermute | solution.py:23
  81.5 3.6 %collective-permute-start.4 = (f32[8,16,128]{2,1,0:T(8,128)S(1)}, f32[8,16,128]{2,1,0:T(8,128)S(1)}, u32[]{:S(2)}, u32[]{:S(2)}) collective-permute-start(f32[8,16,128]{2,1,0:T(8,128)S(1)} %get-tuple-element.15), channel_id=1, source_target_pairs={{0,2},{2,4},{4,6},{1,3},{3,5},{5,7},{8,10},{10,12},{12,14},{9,11},... | collective-permute-start | bytes 196616 | tf_op jit(solution)/shard_map/ppermute | solution.py:20
  83.2 6.2 %collective-permute-start.5 = (f32[8,16,128]{2,1,0:T(8,128)S(1)}, f32[8,16,128]{2,1,0:T(8,128)S(1)}, u32[]{:S(2)}, u32[]{:S(2)}) collective-permute-start(f32[8,16,128]{2,1,0:T(8,128)S(1)} %get-tuple-element.16), channel_id=1, source_target_pairs={{2,0},{4,2},{6,4},{3,1},{5,3},{7,5},{10,8},{12,10},{14,12},{11,9},... | collective-permute-start | bytes 196616 | tf_op jit(solution)/shard_map/ppermute | solution.py:23
  89.4 7.7 %collective-permute-start.6 = (f32[80,8,128]{2,1,0:T(8,128)S(1)}, f32[80,8,128]{2,1,0:T(8,128)S(1)}, u32[]{:S(2)}, u32[]{:S(2)}) collective-permute-start(f32[80,8,128]{2,1,0:T(8,128)S(1)} %get-tuple-element.11), channel_id=1, source_target_pairs={{0,1},{2,3},{4,5},{6,7},{8,9},{10,11},{12,13},{14,15},{16,17},{18,... | collective-permute-start | bytes 983048 | tf_op jit(solution)/shard_map/ppermute | solution.py:20
  92.2 9.1 %collective-permute-start.7 = (f32[80,8,128]{2,1,0:T(8,128)S(1)}, f32[80,8,128]{2,1,0:T(8,128)S(1)}, u32[]{:S(2)}, u32[]{:S(2)}) collective-permute-start(f32[80,8,128]{2,1,0:T(8,128)S(1)} %get-tuple-element.12), channel_id=1, source_target_pairs={{1,0},{3,2},{5,4},{7,6},{9,8},{11,10},{13,12},{15,14},{17,16},{19,... | collective-permute-start | bytes 983048 | tf_op jit(solution)/shard_map/ppermute | solution.py:23
Sparse Core Ops, SparseCore 0:
  105.9 33.3 all-reduce.1
where the time goes:
time: 149 us; the launch traced here: 148 us
  waiting for transfers between devices  62.8 us (42%)
  starting transfers between devices  35.1 us (24%)
  other arithmetic  15.7 us (11%)
  between operations  13.7 us (9%)
  local copies, waits for them, and re-layouts  12.2 us (8%)
  matrix products  8.59 us (6%)
    psum x1, waiting for transfers between devices, local(): logsum = lax.psum(log_term, 'view')  33.5 us
    ppermute x4, waiting for transfers between devices, with_halo(): lax.ppermute(lax.slice_in_dim(block, 0, width, axis=dim), axis, backward)  12.7 us
    ppermute x4, starting transfers between devices, with_halo(): lax.ppermute(lax.slice_in_dim(block, block.shape[dim] - width, None, axis...  12.2 us
    ppermute x4, waiting for transfers between devices, with_halo(): lax.ppermute(lax.slice_in_dim(block, block.shape[dim] - width, None, axis...  11.8 us
    all_to_all x1, starting transfers between devices, local(): lax.all_to_all(send_weight.reshape(bricks, capacity), ('bx', 'by'), split...  7.31 us
    all_to_all x1, starting transfers between devices, local(): lax.all_to_all(send_meta.reshape(bricks, capacity, 2), ('bx', 'by'), spli...  6.62 us
    ppermute x4, starting transfers between devices, with_halo(): lax.ppermute(lax.slice_in_dim(block, 0, width, axis=dim), axis, backward)  5.35 us
    all_to_all x1, starting transfers between devices, local(): lax.all_to_all(send_rows.reshape(bricks, capacity, PV), ('bx', 'by'), spl...  3.56 us
  transfers between devices with their start and end apart: 12, of which 9 were waited for; matrix products, arithmetic and copies ran while one was open for 16% of the time, Pallas kernels for 0%

commit v1 on v0

--- a/solution.py
+++ b/solution.py
@@ -125,7 +125,7 @@
     padded_ratio = with_halo(ratio_field, (("bx", 0), ("by", 1)), R)
     correction = separable(padded_ratio, norm_x[::-1], norm_y[::-1], norm_z[::-1])
     log_term = jnp.log(correction)
-    logsum = lax.psum(log_term, "view")
+    logsum = jnp.sum(lax.all_gather(log_term, "view"), axis=0)
     return estimate * jnp.exp(logsum)
 
 

time: 149 us -> 139 us (0.933)
  waiting for transfers between devices: 62.8 us -> 52 us
    psum x1 -> x0, waiting for transfers between devices: 33.5 us -> none  [local(): logsum = lax.psum(log_term, 'view')]
    all_gather x0 -> x1, waiting for transfers between devices: none -> 22.7 us  [local(): logsum = jnp.sum(lax.all_gather(log_term, 'view'), axis=0)]
    reduce_sum x0 -> x1, other arithmetic: none -> 1.79 us  [local(): logsum = jnp.sum(lax.all_gather(log_term, 'view'), axis=0)]
  transfers between devices with their start and end apart: 12 -> 12, of which waited for: 9 -> 9; matrix products, arithmetic and copies ran while one was open for 16% -> 17% of each run, Pallas kernels for 0% -> 0%
where the time goes in v1:
time: 139 us; the launch traced here: 138 us
  waiting for transfers between devices  52 us (37%)
  starting transfers between devices  35.1 us (25%)
  other arithmetic  16.4 us (12%)
  between operations  13.7 us (10%)
  local copies, waits for them, and re-layouts  12.2 us (9%)
  matrix products  8.59 us (6%)
    all_gather x1, waiting for transfers between devices, local(): logsum = jnp.sum(lax.all_gather(log_term, 'view'), axis=0)  22.7 us
    ppermute x4, waiting for transfers between devices, with_halo(): lax.ppermute(lax.slice_in_dim(block, 0, width, axis=dim), axis, backward)  12.7 us
    ppermute x4, starting transfers between devices, with_halo(): lax.ppermute(lax.slice_in_dim(block, block.shape[dim] - width, None, axis...  12.2 us
    ppermute x4, waiting for transfers between devices, with_halo(): lax.ppermute(lax.slice_in_dim(block, block.shape[dim] - width, None, axis...  11.8 us
    all_to_all x1, starting transfers between devices, local(): lax.all_to_all(send_weight.reshape(bricks, capacity), ('bx', 'by'), split...  7.31 us
    all_to_all x1, starting transfers between devices, local(): lax.all_to_all(send_meta.reshape(bricks, capacity, 2), ('bx', 'by'), spli...  6.62 us
    ppermute x4, starting transfers between devices, with_halo(): lax.ppermute(lax.slice_in_dim(block, 0, width, axis=dim), axis, backward)  5.35 us
    all_to_all x1, starting transfers between devices, local(): lax.all_to_all(send_rows.reshape(bricks, capacity, PV), ('bx', 'by'), spl...  3.56 us
  transfers between devices with their start and end apart: 12, of which 9 were waited for; matrix products, arithmetic and copies ran while one was open for 17% of the time, Pallas kernels for 0%

profile of v1, /device:TPU:0, one launch (start us, length us, event | category | flops | bytes accessed | tf_op | source)
XLA Modules:
  0.0 138.0 jit_solution(13094422944186644087)
XLA Ops:
  6.5 0.7 fusion.26
  8.1 0.8 fusion.23
  8.9 0.7 compare_select_fusion
  9.6 1.6 %scatter_custom_fusion.2 = f32[512]{0:T(512)S(1)} fusion(s32[256]{0:T(256)S(1)} %bitcast.83, f32[256]{0:T(256)} %bitcast.91, f32[]{:T(128)} %constant.22.clone.1), kind=kCustom, calls=%fused_computation.64 | custom fusion | bytes 2560 | tf_op jit(solution)/shard_map/scatter | solution.py:83
  11.1 0.7 all_to_all.14
  11.8 7.3 %all-to-all-start.2 = ((f32[8,1,64]{2,1,0:T(1,128)}), f32[8,1,64]{2,1,0:T(1,128)S(1)}, u32[]{:S(2)}, u32[]{:S(2)}) async-start(f32[8,1,64]{2,1,0:T(1,128)} %all_to_all.14), calls=%async_computation.2 | async-start | bytes 8192 | tf_op jit(solution)/shard_map/all_to_all | solution.py:99
  19.1 0.9 fusion.34
  20.0 3.9 %collective-permute-start = (f32[8,16,128]{2,0,1:T(8,128)S(1)}, f32[8,16,128]{2,0,1:T(8,128)S(1)}, u32[]{:S(2)}, u32[]{:S(2)}) collective-permute-start(f32[8,16,128]{2,0,1:T(8,128)S(1)} %copy.60), channel_id=1, source_target_pairs={{0,2},{2,4},{4,6},{1,3},{3,5},{5,7},{8,10},{10,12},{12,14},{9,11},... | collective-permute-start | bytes 196616 | tf_op jit(solution)/shard_map/ppermute | solution.py:20
  24.0 1.3 collective-permute-start.1
  25.3 1.3 reduce_sum.101
  26.6 0.7 reverse.9
  27.3 1.3 reduce_sum.106
  28.6 0.7 reverse.10
  29.3 1.3 reduce_sum.108
  30.6 0.7 reverse.11
  31.4 1.3 broadcast_divide_fusion.4
  32.7 1.2 broadcast_divide_fusion.2
  33.9 1.3 broadcast_divide_fusion
  36.0 0.7 pad_add_fusion
  36.8 1.2 scatter_custom_fusion
  38.2 0.7 reshape.214
  38.9 6.6 %all-to-all-start = ((s32[8,1,128]{2,1,0:T(1,128)}), s32[8,1,128]{2,1,0:T(1,128)S(1)}, u32[]{:S(2)}, u32[]{:S(2)}) async-start(s32[8,1,128]{2,1,0:T(1,128)} %reshape.214), calls=%async_computation | async-start | bytes 8192 | tf_op jit(solution)/shard_map/all_to_all | solution.py:92
  45.6 2.5 %scatter_custom_fusion.1 = f32[512,512]{1,0:T(8,128)} fusion(s32[256]{0:T(256)S(1)} %bitcast.85, f32[1,256,512]{2,1,0:T(8,128)S(1)} %copy-done, f32[]{:T(128)} %constant.22.clone.1), kind=kCustom, calls=%fused_computation.28 | custom fusion | bytes 1572868 | tf_op jit(solution)/shard_map/scatter | solution.py:77
  48.7 0.7 reduce.8
  49.5 2.5 %all-to-all-done = s32[8,1,128]{2,1,0:T(1,128)S(1)} async-done(((s32[8,1,128]{2,1,0:T(1,128)}), s32[8,1,128]{2,1,0:T(1,128)S(1)}, u32[]{:S(2)}, u32[]{:S(2)}) %all-to-all-start) | async-done | bytes 4128 | tf_op jit(solution)/shard_map/all_to_all | solution.py:92
  51.9 3.6 %all-to-all-start.1 = ((f32[8,64,512]{2,1,0:T(8,128)}), f32[8,64,512]{2,1,0:T(8,128)S(1)}, u32[]{:S(2)}, u32[]{:S(2)}) async-start(f32[8,64,512]{2,1,0:T(8,128)} %bitcast.14), calls=%async_computation.1 | async-start | bytes 2097152 | tf_op jit(solution)/shard_map/all_to_all | solution.py:85
  56.0 0.7 reduce.9
  57.1 3.9 %collective-permute-start.2 = (f32[80,8,128]{2,0,1:T(8,128)S(1)}, f32[80,8,128]{2,0,1:T(8,128)S(1)}, u32[]{:S(2)}, u32[]{:S(2)}) collective-permute-start(f32[80,8,128]{2,0,1:T(8,128)S(1)} %get-tuple-element.13), channel_id=1, source_target_pairs={{0,1},{2,3},{4,5},{6,7},{8,9},{10,11},{12,13},{14,15},{16,17},{18,... | collective-permute-start | bytes 983048 | tf_op jit(solution)/shard_map/ppermute | solution.py:20
  61.0 1.3 collective-permute-start.3
  63.1 7.8 %collective-permute-done.2 = f32[80,8,128]{2,0,1:T(8,128)S(1)} collective-permute-done((f32[80,8,128]{2,0,1:T(8,128)S(1)}, f32[80,8,128]{2,0,1:T(8,128)S(1)}, u32[]{:S(2)}, u32[]{:S(2)}) %collective-permute-start.2) | collective-permute-done | bytes 327712 | tf_op jit(solution)/shard_map/ppermute | solution.py:20
  70.8 4.3 %collective-permute-done.3 = f32[80,8,128]{2,0,1:T(8,128)S(1)} collective-permute-done((f32[80,8,128]{2,0,1:T(8,128)S(1)}, f32[80,8,128]{2,0,1:T(8,128)S(1)}, u32[]{:S(2)}, u32[]{:S(2)}) %collective-permute-start.3) | collective-permute-done | bytes 327712 | tf_op jit(solution)/shard_map/ppermute | solution.py:23
  75.2 1.0 fusion
  76.2 1.3 convolution_bitcast_fusion.1
  77.5 2.3 %all-to-all-done.1 = f32[8,64,512]{2,1,0:T(8,128)S(1)} async-done(((f32[8,64,512]{2,1,0:T(8,128)}), f32[8,64,512]{2,1,0:T(8,128)S(1)}, u32[]{:S(2)}, u32[]{:S(2)}) %all-to-all-start.1) | async-done | bytes 1048608 | tf_op jit(solution)/shard_map/all_to_all | solution.py:85
  79.9 0.7 fusion.8
  81.5 1.7 %collective-permute-start.4 = (f32[8,16,128]{2,1,0:T(8,128)S(1)}, f32[8,16,128]{2,1,0:T(8,128)S(1)}, u32[]{:S(2)}, u32[]{:S(2)}) collective-permute-start(f32[8,16,128]{2,1,0:T(8,128)S(1)} %get-tuple-element.15), channel_id=1, source_target_pairs={{0,2},{2,4},{4,6},{1,3},{3,5},{5,7},{8,10},{10,12},{12,14},{9,11},... | collective-permute-start | bytes 196616 | tf_op jit(solution)/shard_map/ppermute | solution.py:20
  83.2 1.3 collective-permute-start.5
  85.1 4.3 %collective-permute-done.5 = f32[8,16,128]{2,1,0:T(8,128)S(1)} collective-permute-done((f32[8,16,128]{2,1,0:T(8,128)S(1)}, f32[8,16,128]{2,1,0:T(8,128)S(1)}, u32[]{:S(2)}, u32[]{:S(2)}) %collective-permute-start.5) | collective-permute-done | bytes 65568 | tf_op jit(solution)/shard_map/ppermute | solution.py:23
  89.4 2.7 %collective-permute-start.6 = (f32[80,8,128]{2,1,0:T(8,128)S(1)}, f32[80,8,128]{2,1,0:T(8,128)S(1)}, u32[]{:S(2)}, u32[]{:S(2)}) collective-permute-start(f32[80,8,128]{2,1,0:T(8,128)S(1)} %get-tuple-element.11), channel_id=1, source_target_pairs={{0,1},{2,3},{4,5},{6,7},{8,9},{10,11},{12,13},{14,15},{16,17},{18,... | collective-permute-start | bytes 983048 | tf_op jit(solution)/shard_map/ppermute | solution.py:20
  92.2 1.5 %collective-permute-start.7 = (f32[80,8,128]{2,1,0:T(8,128)S(1)}, f32[80,8,128]{2,1,0:T(8,128)S(1)}, u32[]{:S(2)}, u32[]{:S(2)}) collective-permute-start(f32[80,8,128]{2,1,0:T(8,128)S(1)} %get-tuple-element.12), channel_id=1, source_target_pairs={{1,0},{3,2},{5,4},{7,6},{9,8},{11,10},{13,12},{15,14},{17,16},{19,... | collective-permute-start | bytes 983048 | tf_op jit(solution)/shard_map/ppermute | solution.py:23
  93.6 3.5 %collective-permute-done.6 = f32[80,8,128]{2,1,0:T(8,128)S(1)} collective-permute-done((f32[80,8,128]{2,1,0:T(8,128)S(1)}, f32[80,8,128]{2,1,0:T(8,128)S(1)}, u32[]{:S(2)}, u32[]{:S(2)}) %collective-permute-start.6) | collective-permute-done | bytes 327712 | tf_op jit(solution)/shard_map/ppermute | solution.py:20
  97.1 4.1 %collective-permute-done.7 = f32[80,8,128]{2,1,0:T(8,128)S(1)} collective-permute-done((f32[80,8,128]{2,1,0:T(8,128)S(1)}, f32[80,8,128]{2,1,0:T(8,128)S(1)}, u32[]{:S(2)}, u32[]{:S(2)}) %collective-permute-start.7) | collective-permute-done | bytes 327712 | tf_op jit(solution)/shard_map/ppermute | solution.py:23
  101.4 1.8 %fusion.6 = f32[64,32,128]{2,0,1:T(8,128)S(1)} fusion(f32[80,32,128]{2,1,0:T(8,128)S(1)} %pad_maximum_fusion, f32[64,80]{1,0:T(8,128)S(1)} %get-tuple-element.7), kind=kOutput, calls=%fused_computation.13 | convolution fusion | flops 251658240 | bytes 2379776 | tf_op jit(solution)/shard_map/xe,eyz->xyz/dot_general | solution.py:39
  103.1 1.3 convolution_bitcast_fusion
  104.4 1.4 convolution_log_fusion
  105.8 22.7 %all-gather.3.cloned.1.call-done = f32[256,16,128]{2,1,0:T(8,128)} async-done(((f32[64,16,128]{2,1,0:T(8,128)}), f32[256,16,128]{2,1,0:T(8,128)}) %all-gather.3.cloned.1.call-update) | async-done | bytes 2097168 | tf_op jit(solution)/shard_map/all_gather | solution.py:128
  128.5 1.8 %reduce_sum.112 = f32[64,16,128]{2,1,0:T(8,128)S(1)} reduce(f32[4,64,16,128]{3,2,1,0:T(8,128)} %bitcast.70, f32[]{:T(128)} %constant.22.clone.1), dimensions={0}, to_apply=%region_15.16 | reduce | flops 393216 | bytes 2621444 | tf_op jit(solution)/shard_map/reduce_sum | solution.py:128
  130.3 0.9 exponential_multiply_fusion
  (45 shorter events, 6.1 us)
Async XLA Ops:
  6.5 39.1 %copy-start = (f32[1,256,512]{2,1,0:T(8,128)S(1)}, f32[1,256,512]{2,1,0:T(8,128)}, u32[]{:S(2)}) copy-start(f32[1,256,512]{2,1,0:T(8,128)} %param.10) | copy-start | bytes 1572868
  11.8 27.1 %all-to-all-start.2 = ((f32[8,1,64]{2,1,0:T(1,128)}), f32[8,1,64]{2,1,0:T(1,128)S(1)}, u32[]{:S(2)}, u32[]{:S(2)}) async-start(f32[8,1,64]{2,1,0:T(1,128)} %all_to_all.14), calls=%async_computation.2 | async-start | bytes 8192 | tf_op jit(solution)/shard_map/all_to_all | solution.py:99
  20.0 36.9 %collective-permute-start = (f32[8,16,128]{2,0,1:T(8,128)S(1)}, f32[8,16,128]{2,0,1:T(8,128)S(1)}, u32[]{:S(2)}, u32[]{:S(2)}) collective-permute-start(f32[8,16,128]{2,0,1:T(8,128)S(1)} %copy.60), channel_id=1, source_target_pairs={{0,2},{2,4},{4,6},{1,3},{3,5},{5,7},{8,10},{10,12},{12,14},{9,11},... | collective-permute-start | bytes 196616 | tf_op jit(solution)/shard_map/ppermute | solution.py:20
  24.0 33.1 %collective-permute-start.1 = (f32[8,16,128]{2,0,1:T(8,128)S(1)}, f32[8,16,128]{2,0,1:T(8,128)S(1)}, u32[]{:S(2)}, u32[]{:S(2)}) collective-permute-start(f32[8,16,128]{2,0,1:T(8,128)S(1)} %copy.61), channel_id=1, source_target_pairs={{2,0},{4,2},{6,4},{3,1},{5,3},{7,5},{10,8},{12,10},{14,12},{11,9},... | collective-permute-start | bytes 196616 | tf_op jit(solution)/shard_map/ppermute | solution.py:23
  38.9 13.0 %all-to-all-start = ((s32[8,1,128]{2,1,0:T(1,128)}), s32[8,1,128]{2,1,0:T(1,128)S(1)}, u32[]{:S(2)}, u32[]{:S(2)}) async-start(s32[8,1,128]{2,1,0:T(1,128)} %reshape.214), calls=%async_computation | async-start | bytes 8192 | tf_op jit(solution)/shard_map/all_to_all | solution.py:92
  48.1 8.8 %copy-start.1 = (f32[64,16,128]{2,1,0:T(8,128)S(1)}, f32[64,16,128]{2,1,0:T(8,128)}, u32[]{:S(2)}) copy-start(f32[64,16,128]{2,1,0:T(8,128)} %param.9) | copy-start | bytes 1572868
  51.9 27.9 %all-to-all-start.1 = ((f32[8,64,512]{2,1,0:T(8,128)}), f32[8,64,512]{2,1,0:T(8,128)S(1)}, u32[]{:S(2)}, u32[]{:S(2)}) async-start(f32[8,64,512]{2,1,0:T(8,128)} %bitcast.14), calls=%async_computation.1 | async-start | bytes 2097152 | tf_op jit(solution)/shard_map/all_to_all | solution.py:85
  55.5 73.0 %all-gather.3.cloned.1.call-start = ((), (), s32[]{:S(2)}) async-start(), calls=%async_computation.3 | async-start | bytes 2621440 | tf_op jit(solution)/shard_map/all_gather | solution.py:128
  57.1 13.7 %collective-permute-start.2 = (f32[80,8,128]{2,0,1:T(8,128)S(1)}, f32[80,8,128]{2,0,1:T(8,128)S(1)}, u32[]{:S(2)}, u32[]{:S(2)}) collective-permute-start(f32[80,8,128]{2,0,1:T(8,128)S(1)} %get-tuple-element.13), channel_id=1, source_target_pairs={{0,1},{2,3},{4,5},{6,7},{8,9},{10,11},{12,13},{14,15},{16,17},{18,... | collective-permute-start | bytes 983048 | tf_op jit(solution)/shard_map/ppermute | solution.py:20
  61.0 14.1 %collective-permute-start.3 = (f32[80,8,128]{2,0,1:T(8,128)S(1)}, f32[80,8,128]{2,0,1:T(8,128)S(1)}, u32[]{:S(2)}, u32[]{:S(2)}) collective-permute-start(f32[80,8,128]{2,0,1:T(8,128)S(1)} %get-tuple-element.14), channel_id=1, source_target_pairs={{1,0},{3,2},{5,4},{7,6},{9,8},{11,10},{13,12},{15,14},{17,16},{19,... | collective-permute-start | bytes 983048 | tf_op jit(solution)/shard_map/ppermute | solution.py:23
  81.5 3.6 %collective-permute-start.4 = (f32[8,16,128]{2,1,0:T(8,128)S(1)}, f32[8,16,128]{2,1,0:T(8,128)S(1)}, u32[]{:S(2)}, u32[]{:S(2)}) collective-permute-start(f32[8,16,128]{2,1,0:T(8,128)S(1)} %get-tuple-element.15), channel_id=1, source_target_pairs={{0,2},{2,4},{4,6},{1,3},{3,5},{5,7},{8,10},{10,12},{12,14},{9,11},... | collective-permute-start | bytes 196616 | tf_op jit(solution)/shard_map/ppermute | solution.py:20
  83.2 6.2 %collective-permute-start.5 = (f32[8,16,128]{2,1,0:T(8,128)S(1)}, f32[8,16,128]{2,1,0:T(8,128)S(1)}, u32[]{:S(2)}, u32[]{:S(2)}) collective-permute-start(f32[8,16,128]{2,1,0:T(8,128)S(1)} %get-tuple-element.16), channel_id=1, source_target_pairs={{2,0},{4,2},{6,4},{3,1},{5,3},{7,5},{10,8},{12,10},{14,12},{11,9},... | collective-permute-start | bytes 196616 | tf_op jit(solution)/shard_map/ppermute | solution.py:23
  89.4 7.7 %collective-permute-start.6 = (f32[80,8,128]{2,1,0:T(8,128)S(1)}, f32[80,8,128]{2,1,0:T(8,128)S(1)}, u32[]{:S(2)}, u32[]{:S(2)}) collective-permute-start(f32[80,8,128]{2,1,0:T(8,128)S(1)} %get-tuple-element.11), channel_id=1, source_target_pairs={{0,1},{2,3},{4,5},{6,7},{8,9},{10,11},{12,13},{14,15},{16,17},{18,... | collective-permute-start | bytes 983048 | tf_op jit(solution)/shard_map/ppermute | solution.py:20
  92.2 9.1 %collective-permute-start.7 = (f32[80,8,128]{2,1,0:T(8,128)S(1)}, f32[80,8,128]{2,1,0:T(8,128)S(1)}, u32[]{:S(2)}, u32[]{:S(2)}) collective-permute-start(f32[80,8,128]{2,1,0:T(8,128)S(1)} %get-tuple-element.12), channel_id=1, source_target_pairs={{1,0},{3,2},{5,4},{7,6},{9,8},{11,10},{13,12},{15,14},{17,16},{19,... | collective-permute-start | bytes 983048 | tf_op jit(solution)/shard_map/ppermute | solution.py:23
Sparse Core Ops, SparseCore 0:
  105.9 22.5 all-gather.2
